TPU v7x, 512 devices: a whole 4x8x8 slice. The times are simulated.
512 devices in a mesh: grp: 16 (over z, core), dev: 32 (over y, x).
Axes of the slice: x: 4, y: 8, z: 8, core: 2. Of those that a mesh axis runs over, the one named last changes fastest.
Arguments:
- stored_tiles: float32 [512, 33, 128, 128], P(('grp', 'dev')), may hold values from -0.22097087 to 0.22097087, as said below
- tile_flags: int32 [512, 33], P(('grp', 'dev')), may hold values from 0 to 1, as said below
- orbitals: float32 [65536, 256], P(('grp', 'dev')), may hold values from -6 to 6
Outputs:
- product: float32 [65536, 256], P(('grp', 'dev'))
Inputs may be any that keep to these rules, and one draw needn't show every extreme that they name: tile_flags[p, s] is 1 at s = p mod 32, 0 for s below that, and 0 at s = 32 in the last 32 block rows. `stored_tiles`: the tile at slot p mod 32 of block row p is symmetric.
All inputs are finite; a program needn't handle non-finite values.
Results may differ from a plain program's by a relative error of at most 0.000075.
Values sent between devices are 32-bit elements; how exact they have to be, the bound alone decides.
A program may use at most 64 MiB of HBM per device.

v0:
```python
import jax
import jax.numpy as jnp
from jax import lax
from jax.sharding import PartitionSpec as P


def shifted(shard, axis, by):
    count = lax.axis_size(axis)
    pairs = [(i, i + by) for i in range(count) if 0 <= i + by < count]
    return lax.ppermute(shard, axis, pairs)


def per_device(stored_tiles, tile_flags, orbitals):
    highest = lax.Precision.HIGHEST
    group_width = lax.axis_size("dev")
    own_index = lax.axis_index("dev")
    tile_order = stored_tiles.shape[2]
    columns = orbitals.shape[1]
    slot_index = lax.broadcasted_iota(jnp.int32, (group_width,), 0)
    flags_float = tile_flags[0].astype(jnp.float32)
    blocks = stored_tiles[0] * flags_float[:, None, None]
    in_group = blocks[:group_width]
    next_tile = blocks[group_width]
    beside = in_group * (slot_index != own_index).astype(jnp.float32)[:, None, None]
    piece_rows = lax.all_gather(orbitals, "dev", axis=0, tiled=True)
    num_slots = piece_rows.shape[0] // tile_order
    x_rows = piece_rows.reshape(num_slots, tile_order, columns)
    product = jnp.einsum("sij,sjk->ik", in_group, x_rows, precision=highest)
    row_count = lax.axis_size("dev") * orbitals.shape[0]
    terms = jnp.einsum("sji,jk->sik", beside, orbitals, precision=highest)
    product = product + lax.psum_scatter(
        terms.reshape(row_count, columns), "dev", scatter_dimension=0, tiled=True
    )
    following = shifted(orbitals, "grp", -1)
    product = product + jnp.dot(next_tile, following, precision=highest)
    upward = jnp.einsum("ji,jk->ik", next_tile, orbitals, precision=highest)
    product = product + shifted(upward, "grp", 1)
    return product


def solution(mesh):
    in_specs = (
        P(("grp", "dev"), None, None, None),
        P(("grp", "dev"), None),
        P(("grp", "dev"), None),
    )
    out_specs = P(("grp", "dev"), None)
    return jax.shard_map(
        per_device, mesh=mesh, in_specs=in_specs, out_specs=out_specs, check_vma=False
    )
```

profile of v0, /device:TPU:16, one launch (start us, length us, event | category | flops | bytes accessed | tf_op | source)
XLA Modules:
  0.0 342.0 jit_solution(7017481486420995727)
XLA Ops:
  6.5 0.0 all-gather.2.cloned.1.call-start
  6.5 0.7 all-gather.2.cloned.1.call-update
  7.3 0.0 reduce-scatter.2.cloned.1.call-start
  7.3 0.7 convert_bitcast_fusion
  8.0 0.0 copy-start
  8.0 1.8 bitcast_multiply_fusion
  9.8 0.0 copy-done
  9.8 5.7 %fusion = f32[32,128,256]{2,1,0:T(8,128)} fusion(f32[33,128,128]{2,1,0:T(8,128)S(1)} %bitcast_multiply_fusion, f32[32]{0:T(128)S(1)} %compare_convert_fusion, f32[128,256]{1,0:T(8,128)S(1)} %copy-done), kind=kOutput, calls=%fused_computation.2 | convolution fusion | flops 1611137024 | bytes 6423040 | tf_op jit(solution)/shard_map/sji,jk->sik/dot_general | solution.py:30
  15.5 0.0 reduce-scatter.2.cloned.1.call-update
  15.6 1.3 collective-permute-start
  16.9 0.3 fusion.5
  17.2 3.0 collective-permute-start.1
  20.2 80.8 %all-gather.2.cloned.1.call-done = f32[4096,256]{1,0:T(8,128)} async-done(((f32[128,256]{1,0:T(8,128)}), f32[4096,256]{1,0:T(8,128)}) %all-gather.2.cloned.1.call-update) | async-done | bytes 4194320 | tf_op jit(solution)/shard_map/all_gather | solution.py:25
  101.0 229.2 %reduce-scatter.2.cloned.1.call-done = f32[128,256]{1,0:T(8,128)} async-done(((f32[4096,256]{1,0:T(8,128)}), f32[128,256]{1,0:T(8,128)}) %reduce-scatter.2.cloned.1.call-update) | async-done | bytes 131088 | tf_op jit(solution)/shard_map/reduce_scatter | solution.py:31
  330.2 3.9 %fusion.2 = f32[128,256]{1,0:T(8,128)S(1)} fusion(f32[128,256]{1,0:T(8,128)} %reduce-scatter.2.cloned.1.call-done, f32[33,128,128]{2,1,0:T(8,128)S(1)} %bitcast_multiply_fusion, f32[32,128,256]{2,1,0:T(8,128)} %bitcast.22), kind=kOutput, calls=%fused_computation.6 | convolution fusion | flops 1610645504 | bytes 6619136 | tf_op jit(solution)/shard_map/sij,sjk->ik/dot_general | solution.py:28
  334.2 0.0 collective-permute-done.1
  334.2 0.0 collective-permute-done
  334.2 0.9 fusion.1
  (1 shorter events, 0.0 us)
Async XLA Ops:
  6.5 94.5 %all-gather.2.cloned.1.call-start = ((), (), s32[]{:S(2)}) async-start(), calls=%async_computation.1 | async-start | bytes 4325376 | tf_op jit(solution)/shard_map/all_gather | solution.py:25
  7.3 323.0 %reduce-scatter.2.cloned.1.call-start = ((), (), s32[]{:S(2)}) async-start(), calls=%async_computation.2 | async-start | bytes 4325376 | tf_op jit(solution)/shard_map/reduce_scatter | solution.py:31
  8.0 1.9 copy-start
  15.6 318.6 %collective-permute-start = (f32[128,256]{1,0:T(8,128)S(1)}, f32[128,256]{1,0:T(8,128)S(1)}, u32[]{:S(2)}, u32[]{:S(2)}) collective-permute-start(f32[128,256]{1,0:T(8,128)S(1)} %copy-done), channel_id=1, source_target_pairs={{32,0},{64,32},{96,64},{128,96},{160,128},{192,160},{224,192},{256... | collective-permute-start | bytes 393224 | tf_op jit(solution)/shard_map/ppermute | solution.py:10
  17.2 317.0 %collective-permute-start.1 = (f32[128,256]{1,0:T(8,128)S(1)}, f32[128,256]{1,0:T(8,128)S(1)}, u32[]{:S(2)}, u32[]{:S(2)}) collective-permute-start(f32[128,256]{1,0:T(8,128)S(1)} %fusion.5), channel_id=1, source_target_pairs={{0,32},{32,64},{64,96},{96,128},{128,160},{160,192},{192,224},{224... | collective-permute-start | bytes 393224 | tf_op jit(solution)/shard_map/ppermute | solution.py:10
Sparse Core Ops, SparseCore 0:
  10.5 90.4 all-gather.1
  105.5 224.7 reduce-scatter.1
where the time goes:
time: 342 us
  waiting for transfers between devices  311 us (91%)
  between operations  13.5 us (4%)
  matrix products  10.9 us (3%)
  starting transfers between devices  4.37 us (1%)
    reduce_scatter x1, waiting for transfers between devices, per_device(): lax.psum_scatter(terms.reshape(row_count, columns), 'dev', scatter_dimens...  229 us
    all_gather x1, waiting for transfers between devices, per_device(): piece_rows = lax.all_gather(orbitals, 'dev', axis=0, tiled=True)  80.8 us
  transfers between devices with their start and end apart: 4, of which 2 were waited for; matrix products, arithmetic and copies ran while one was open for 4% of the time, Pallas kernels for 0%

commit v1 on v0

--- a/solution.py
+++ b/solution.py
@@ -22,7 +22,9 @@
     in_group = blocks[:group_width]
     next_tile = blocks[group_width]
     beside = in_group * (slot_index != own_index).astype(jnp.float32)[:, None, None]
-    piece_rows = lax.all_gather(orbitals, "dev", axis=0, tiled=True)
+    piece_rows = jnp.concatenate(
+        lax.all_to_all(jnp.stack([orbitals] * lax.axis_size("dev")), "dev", 0, 0), axis=0
+    )
     num_slots = piece_rows.shape[0] // tile_order
     x_rows = piece_rows.reshape(num_slots, tile_order, columns)
     product = jnp.einsum("sij,sjk->ik", in_group, x_rows, precision=highest)

time: 342 us -> 290 us (0.85)
  waiting for transfers between devices: 311 us -> 246 us
  starting transfers between devices: 4.37 us -> 14.5 us
    all_to_all x0 -> x1, waiting for transfers between devices: none -> 102 us  [per_device(): lax.all_to_all(jnp.stack([orbitals] * lax.axis_size('dev')), 'dev', 0, 0)]
    reduce_scatter x1, waiting for transfers between devices: 229 us -> 144 us  [per_device(): lax.psum_scatter(terms.reshape(row_count, columns), 'dev', scatter_dimens...]
    all_gather x1 -> x0, waiting for transfers between devices: 80.8 us -> none  [per_device(): piece_rows = lax.all_gather(orbitals, 'dev', axis=0, tiled=True)]
    all_to_all x0 -> x1, starting transfers between devices: none -> 10.2 us  [per_device(): lax.all_to_all(jnp.stack([orbitals] * lax.axis_size('dev')), 'dev', 0, 0)]
  transfers between devices with their start and end apart: 4 -> 4, of which waited for: 2 -> 2; matrix products, arithmetic and copies ran while one was open for 4% -> 2% of each run, Pallas kernels for 0% -> 0%
where the time goes in v1:
time: 290 us
  waiting for transfers between devices  246 us (85%)
  starting transfers between devices  14.5 us (5%)
  between operations  13.5 us (5%)
  matrix products  10.8 us (4%)
    reduce_scatter x1, waiting for transfers between devices, per_device(): lax.psum_scatter(terms.reshape(row_count, columns), 'dev', scatter_dimens...  144 us
    all_to_all x1, waiting for transfers between devices, per_device(): lax.all_to_all(jnp.stack([orbitals] * lax.axis_size('dev')), 'dev', 0, 0)  102 us
    all_to_all x1, starting transfers between devices, per_device(): lax.all_to_all(jnp.stack([orbitals] * lax.axis_size('dev')), 'dev', 0, 0)  10.2 us
  transfers between devices with their start and end apart: 4, of which 2 were waited for; matrix products, arithmetic and copies ran while one was open for 2% of the time, Pallas kernels for 0%

profile of v1, /device:TPU:16, one launch (start us, length us, event | category | flops | bytes accessed | tf_op | source)
XLA Modules:
  0.0 289.9 jit_solution(5337106617781189020)
XLA Ops:
  6.5 0.0 reduce-scatter.2.cloned.1.call-start
  6.5 0.7 convert_bitcast_fusion
  7.2 0.0 copy-start
  7.2 1.8 bitcast_multiply_fusion
  9.1 0.0 copy-done
  9.1 5.7 %fusion = f32[32,128,256]{2,1,0:T(8,128)} fusion(f32[33,128,128]{2,1,0:T(8,128)S(1)} %bitcast_multiply_fusion, f32[32]{0:T(128)S(1)} %compare_convert_fusion, f32[128,256]{1,0:T(8,128)S(1)} %copy-done), kind=kOutput, calls=%fused_computation.2 | convolution fusion | flops 1611137024 | bytes 6423040 | tf_op jit(solution)/shard_map/sji,jk->sik/dot_general | solution.py:32
  14.7 0.0 reduce-scatter.2.cloned.1.call-update
  14.7 2.4 stack.2
  17.2 10.2 %all-to-all-start = ((f32[32,128,256]{2,1,0:T(8,128)}), f32[32,128,256]{2,1,0:T(8,128)}, u32[]{:S(2)}, u32[]{:S(2)}) async-start(f32[32,128,256]{2,1,0:T(8,128)} %stack.2), calls=%async_computation | async-start | bytes 8388608 | tf_op jit(solution)/shard_map/all_to_all | solution.py:26
  27.4 1.3 collective-permute-start
  28.7 0.3 fusion.5
  29.0 3.0 %collective-permute-start.1 = (f32[128,256]{1,0:T(8,128)S(1)}, f32[128,256]{1,0:T(8,128)S(1)}, u32[]{:S(2)}, u32[]{:S(2)}) collective-permute-start(f32[128,256]{1,0:T(8,128)S(1)} %fusion.5), channel_id=1, source_target_pairs={{0,32},{32,64},{64,96},{96,128},{128,160},{160,192},{192,224},{224... | collective-permute-start | bytes 393224 | tf_op jit(solution)/shard_map/ppermute | solution.py:10
  32.0 102.3 %all-to-all-done = f32[32,128,256]{2,1,0:T(8,128)} async-done(((f32[32,128,256]{2,1,0:T(8,128)}), f32[32,128,256]{2,1,0:T(8,128)}, u32[]{:S(2)}, u32[]{:S(2)}) %all-to-all-start) | async-done | bytes 4194336 | tf_op jit(solution)/shard_map/all_to_all | solution.py:26
  134.3 143.9 %reduce-scatter.2.cloned.1.call-done = f32[128,256]{1,0:T(8,128)} async-done(((f32[4096,256]{1,0:T(8,128)}), f32[128,256]{1,0:T(8,128)}) %reduce-scatter.2.cloned.1.call-update) | async-done | bytes 131088 | tf_op jit(solution)/shard_map/reduce_scatter | solution.py:33
  278.2 3.9 %fusion.2 = f32[128,256]{1,0:T(8,128)S(1)} fusion(f32[128,256]{1,0:T(8,128)} %reduce-scatter.2.cloned.1.call-done, f32[33,128,128]{2,1,0:T(8,128)S(1)} %bitcast_multiply_fusion, f32[32,128,256]{2,1,0:T(8,128)} %all-to-all-done), kind=kOutput, calls=%fused_computation.6 | convolution fusion | flops 1610645504 | bytes 6619136 | tf_op jit(solution)/shard_map/sij,sjk->ik/dot_general | solution.py:30
  282.1 0.0 collective-permute-done.1
  282.1 0.0 collective-permute-done
  282.2 0.9 fusion.1
  (1 shorter events, 0.0 us)
Async XLA Ops:
  6.5 271.7 %reduce-scatter.2.cloned.1.call-start = ((), (), s32[]{:S(2)}) async-start(), calls=%async_computation.2 | async-start | bytes 4325376 | tf_op jit(solution)/shard_map/reduce_scatter | solution.py:33
  7.2 1.9 copy-start
  17.2 117.1 %all-to-all-start = ((f32[32,128,256]{2,1,0:T(8,128)}), f32[32,128,256]{2,1,0:T(8,128)}, u32[]{:S(2)}, u32[]{:S(2)}) async-start(f32[32,128,256]{2,1,0:T(8,128)} %stack.2), calls=%async_computation | async-start | bytes 8388608 | tf_op jit(solution)/shard_map/all_to_all | solution.py:26
  27.4 254.8 %collective-permute-start = (f32[128,256]{1,0:T(8,128)S(1)}, f32[128,256]{1,0:T(8,128)S(1)}, u32[]{:S(2)}, u32[]{:S(2)}) collective-permute-start(f32[128,256]{1,0:T(8,128)S(1)} %copy-done), channel_id=1, source_target_pairs={{32,0},{64,32},{96,64},{128,96},{160,128},{192,160},{224,192},{256... | collective-permute-start | bytes 393224 | tf_op jit(solution)/shard_map/ppermute | solution.py:10
  29.0 253.2 %collective-permute-start.1 = (f32[128,256]{1,0:T(8,128)S(1)}, f32[128,256]{1,0:T(8,128)S(1)}, u32[]{:S(2)}, u32[]{:S(2)}) collective-permute-start(f32[128,256]{1,0:T(8,128)S(1)} %fusion.5), channel_id=1, source_target_pairs={{0,32},{32,64},{64,96},{96,128},{128,160},{160,192},{192,224},{224... | collective-permute-start | bytes 393224 | tf_op jit(solution)/shard_map/ppermute | solution.py:10
Sparse Core Ops, SparseCore 0:
  14.9 263.2 reduce-scatter.1
